TPU v7x, 128 devices: a whole 4x4x4 slice. The times are simulated.
128 devices in a mesh: rep: 16 (over z, y), shard: 8 (over x, core).
Axes of the slice: x: 4, y: 4, z: 4, core: 2. Of those that a mesh axis runs over, the one named last changes fastest.
Arguments:
- grads: bfloat16 [16, 8, 1024, 1024], P('rep', 'shard'), may hold values from -6 to 6
- master: float32 [8, 256, 1024], P('shard'), may hold values from -4 to 4
- moment_one: float32 [8, 256, 1024], P('shard'), may hold values from -4 to 4
- moment_two: float32 [8, 256, 1024], P('shard'), may hold values from 0.01 to 10
- average: float32 [8, 256, 1024], P('shard'), may hold values from -4 to 4
- tensor_owner: int32 [32], replicated, may hold values from 0 to 7, as said below
- tensor_start: int32 [32], replicated, may hold values from 0 to 1008, as said below
- tensor_rows: int32 [32], replicated, may hold values from 16 to 208, as said below
- tensor_slot: int32 [32], replicated, may hold values from 0 to 240, as said below
Outputs:
- new_params: float32 [1024, 1024], replicated
- master_new: float32 [8, 256, 1024], P('shard')
- moment_one_new: float32 [8, 256, 1024], P('shard')
- moment_two_new: float32 [8, 256, 1024], P('shard')
- average_new: float32 [8, 256, 1024], P('shard')
Inputs may be any that keep to these rules, and one draw needn't show every extreme that they name: `tensor_owner`: every owner holds exactly 4 tensors; one owner's tensors have exactly 256 rows together and no owner's more. `tensor_start`: the tensors cover the window's rows without gaps or intersections. `tensor_rows`: each tensor's rows are a multiple of 16. `tensor_slot`: an owner's tensors fill its buffer rows from 0 upward without gaps or intersections.
All inputs are finite; a program needn't handle non-finite values.
Results may differ from a plain program's by a relative error of at most 0.0003.
Values may be sent and summed in bfloat16 or wider, within the bound.
No kernel may reach another device: no remote copies, remote signals or barrier semaphores. Data moves between devices by JAX's collectives and lax.ppermute only.
A program may use at most 128 MiB of HBM per device.

v0:
```python
import math
import jax
import jax.numpy as jnp
from jax import lax
from jax.sharding import PartitionSpec as P

beta_one = 0.9
beta_two = 0.95
epsilon = 1e-08
learn_rate = 0.01
decay_base = 0.1
average_rate = 0.99
step_count = 10.0
reference_batch = 128.0


def optimizer_step(summed, master, moment_one, moment_two, average, decay_scale):
    moment_one_new = beta_one * moment_one + (1.0 - beta_one) * summed
    moment_two_new = beta_two * moment_two + (1.0 - beta_two) * summed * summed
    corr_one = 1.0 - beta_one**step_count
    corr_two = 1.0 - beta_two**step_count
    update = moment_one_new / corr_one / (jnp.sqrt(moment_two_new / corr_two) + epsilon)
    master_new = master * (1.0 - learn_rate * decay_base * decay_scale) - learn_rate * update
    average_new = average_rate * average + (1.0 - average_rate) * master_new
    return (master_new, moment_one_new, moment_two_new, average_new)


def packed_rows(
    gradient, tensor_owner, tensor_start, tensor_rows, tensor_slot, dest_owner, dest_slot, wire_type
):
    slot_begin = tensor_slot[None, :]
    covered = (
        (dest_owner[:, None] == tensor_owner[None, :])
        & (dest_slot[:, None] >= slot_begin)
        & (dest_slot[:, None] < slot_begin + tensor_rows[None, :])
    )
    offset = tensor_start[None, :] + dest_slot[:, None] - slot_begin
    window_row = jnp.sum(jnp.where(covered, offset, 0), axis=1)
    present = jnp.any(covered, axis=1)
    picked = jnp.take(gradient, window_row, axis=0)
    return jnp.where(present[:, None], picked, jnp.zeros((), wire_type))


def add_sources(received):
    return jnp.sum(received, axis=0, dtype=jnp.float32)


def local(
    grads,
    master,
    moment_one,
    moment_two,
    average,
    tensor_owner,
    tensor_start,
    tensor_rows,
    tensor_slot,
):
    gradient = grads[0, 0]
    owners = lax.axis_size("shard")
    replicas = lax.axis_size("rep")
    capacity = master.shape[1]
    row_width = gradient.shape[1]
    row_total = gradient.shape[0]
    decay_scale = math.sqrt(owners * replicas / reference_batch)
    slot_index = jnp.arange(owners * capacity, dtype=jnp.int32)
    dest_owner = slot_index // capacity
    dest_slot = slot_index % capacity
    window_sum = lax.psum(gradient.astype(jnp.float32), "rep")
    packed = packed_rows(
        window_sum,
        tensor_owner,
        tensor_start,
        tensor_rows,
        tensor_slot,
        dest_owner,
        dest_slot,
        jnp.float32,
    )
    packed = packed.reshape(owners, capacity, row_width)
    summed = add_sources(lax.all_to_all(packed, "shard", split_axis=0, concat_axis=0, tiled=True))
    states = optimizer_step(
        summed, master[0], moment_one[0], moment_two[0], average[0], decay_scale
    )
    updated = states[0]
    row_index = jnp.arange(row_total, dtype=jnp.int32)
    inside = (row_index[:, None] >= tensor_start[None, :]) & (
        row_index[:, None] < (tensor_start + tensor_rows)[None, :]
    )
    target = tensor_owner * capacity + tensor_slot - tensor_start
    destination = jnp.sum(jnp.where(inside, target[None, :] + row_index[:, None], 0), axis=1)
    piece = lax.all_gather(updated, "shard", axis=0, tiled=True)
    within = (destination >= 0) & (destination < piece.shape[0])
    picked = jnp.take(piece, jnp.clip(destination, 0, piece.shape[0] - 1), axis=0)
    new_params = jnp.where(within[:, None], picked, jnp.zeros((row_total, row_width), jnp.float32))
    return (new_params, states[0][None], states[1][None], states[2][None], states[3][None])


def solution(mesh):
    in_specs = (
        P("rep", "shard", None, None),
        P("shard", None, None),
        P("shard", None, None),
        P("shard", None, None),
        P("shard", None, None),
        P(),
        P(),
        P(),
        P(),
    )
    out_specs = (
        P(),
        P("shard", None, None),
        P("shard", None, None),
        P("shard", None, None),
        P("shard", None, None),
    )
    return jax.shard_map(local, mesh=mesh, in_specs=in_specs, out_specs=out_specs, check_vma=False)
```

profile of v0, /device:TPU:1, one launch (start us, length us, event | category | flops | bytes accessed | tf_op | source)
XLA Modules:
  0.0 313.1 jit_solution(11101088858374454357)
XLA Ops:
  7.2 0.0 copy-start.3
  7.2 0.0 copy-start.4
  7.2 0.0 copy-start.5
  7.2 0.0 copy-start.2
  7.2 0.0 all-reduce.2.cloned.1.call-start
  7.3 4.1 %bitcast_convert_fusion = f32[1024,1024]{1,0:T(8,128)} fusion(bf16[1,1,1024,1024]{3,2,1,0:T(8,128)(2,1)} %param.9), kind=kLoop, calls=%fused_computation.4 | loop fusion | flops 1048576 | bytes 6291456 | tf_op jit(solution)/shard_map/convert_element_type | solution.py:69
  11.3 0.0 all-reduce.2.cloned.1.call-update
  11.3 0.0 all-gather.2.cloned.1.call-start
  11.4 0.0 copy-done.3
  11.4 0.0 copy-done.4
  11.4 0.0 copy-done.5
  11.4 0.0 copy-done.2
  11.5 0.2 select_reduce_fusion
  11.6 0.2 fusion.18
  11.9 106.7 %all-reduce.2.cloned.1.call-done = f32[1024,1024]{1,0:T(8,128)} async-done(((f32[1024,1024]{1,0:T(8,128)}), f32[1024,1024]{1,0:T(8,128)}) %all-reduce.2.cloned.1.call-update) | async-done | bytes 4194320 | tf_op jit(solution)/shard_map/psum | solution.py:69
  118.6 13.9 %gather_fusion = f32[2048,1024]{1,0:T(8,128)} fusion(f32[1024,1024]{1,0:T(8,128)} %all-reduce.2.cloned.1.call-done, s32[2048]{0:T(1024)S(1)} %broadcast_clamp_fusion), kind=kCustom, calls=%fused_computation | custom fusion | bytes 16785408 | tf_op jit(solution)/shard_map/jit(_take)/gather | solution.py:40
  132.4 4.0 %select_select_fusion = f32[8,256,1024]{2,1,0:T(8,128)S(1)} fusion(f32[8,256,1024]{2,1,0:T(8,128)} %bitcast.25, pred[8,256]{1,0:T(8,128)(4,1)S(1)} %compare_and_fusion.1, pred[8,256]{1,0:T(8,128)(4,1)S(1)} %broadcast_in_dim.76), kind=kLoop, calls=%fused_computation.2 | loop fusion | flops 4194304 | bytes 16781312 | tf_op jit(solution)/shard_map/jit(_where)/select_n | solution.py:41
  136.4 100.0 %all_to_all.5 = f32[8,256,1024]{2,1,0:T(8,128)} all-to-all(f32[8,256,1024]{2,1,0:T(8,128)S(1)} %select_select_fusion), channel_id=1, replica_groups=mesh['rep'=16,'shard'=8] {'shard'}, dimensions={0} | all-to-all | bytes 16777216 | tf_op jit(solution)/shard_map/all_to_all | solution.py:81
  236.4 0.0 copy-start
  236.4 0.0 copy-start.1
  236.4 4.5 %reduce_sum.37 = f32[256,1024]{1,0:T(8,128)S(1)} reduce(f32[8,256,1024]{2,1,0:T(8,128)} %all_to_all.5, f32[]{:T(128)} %constant.83.clone.1), dimensions={0}, to_apply=%region_4.5 | reduce | flops 1835008 | bytes 9437188 | tf_op jit(solution)/shard_map/reduce_sum | solution.py:45
  241.0 0.0 copy-done
  241.0 0.0 copy-done.1
  241.0 3.0 fusion.6
  243.9 0.0 all-gather.2.cloned.1.call-update
  244.0 0.1 select_reduce_fusion.1
  244.1 4.2 %multiply_add_fusion = (f32[1,256,1024]{2,1,0:T(8,128)}, f32[1,256,1024]{2,1,0:T(8,128)}, f32[1,256,1024]{2,1,0:T(8,128)}, f32[1,256,1024]{2,1,0:T(8,128)}) fusion(f32[1,256,1024]{2,1,0:T(8,128)} %param.13, f32[1,256,1024]{2,1,0:T(8,128)} %param.10, f32[256,1024]{1,0:T(8,128)S(1)} %reduce_sum.37, f32[1,256,1024]{2,1,0:T(8,128)S(1)} %copy-done.1, ...), kind=kLoop, calls=%fused_computation.19 | loop fusion | flops 4456448 | bytes 9437184 | tf_op jit(solution)/shard_map/add | solution.py:24
  248.4 44.1 %all-gather.2.cloned.1.call-done = f32[2048,1024]{1,0:T(8,128)} async-done(((f32[256,1024]{1,0:T(8,128)}), f32[2048,1024]{1,0:T(8,128)}) %all-gather.2.cloned.1.call-update) | async-done | bytes 8388624 | tf_op jit(solution)/shard_map/all_gather | solution.py:92
  292.4 9.7 %gather_fusion.1 = f32[1024,1024]{1,0:T(8,128)} fusion(f32[2048,1024]{1,0:T(8,128)} %all-gather.2.cloned.1.call-done, s32[1024]{0:T(1024)S(1)} %broadcast_clamp_fusion.1), kind=kCustom, calls=%fused_computation.1 | custom fusion | bytes 8392704 | tf_op jit(solution)/shard_map/jit(_take)/gather | solution.py:94
  302.1 4.2 %select_select_fusion.1 = f32[1024,1024]{1,0:T(8,128)} fusion(f32[1024,1024]{1,0:T(8,128)} %gather_fusion.1, pred[1024]{0:T(1024)(128)(4,1)S(1)} %get-tuple-element.10, pred[1024]{0:T(1024)(128)(4,1)S(1)} %get-tuple-element.9), kind=kLoop, calls=%fused_computation.3 | loop fusion | flops 2097152 | bytes 8390656 | tf_op jit(solution)/shard_map/jit(_where)/select_n | solution.py:95
  (11 shorter events, 0.1 us)
Async XLA Ops:
  7.2 4.2 %copy-start.3 = (s32[32]{0:T(128)S(1)}, s32[32]{0:T(128)}, u32[]{:S(2)}) copy-start(s32[32]{0:T(128)} %param.14) | copy-start | bytes 388
  7.2 4.2 %copy-start.4 = (s32[32]{0:T(128)S(1)}, s32[32]{0:T(128)}, u32[]{:S(2)}) copy-start(s32[32]{0:T(128)} %param.15) | copy-start | bytes 388
  7.2 4.2 %copy-start.5 = (s32[32]{0:T(128)S(1)}, s32[32]{0:T(128)}, u32[]{:S(2)}) copy-start(s32[32]{0:T(128)} %param.16) | copy-start | bytes 388
  7.2 4.2 %copy-start.2 = (s32[32]{0:T(128)S(1)}, s32[32]{0:T(128)}, u32[]{:S(2)}) copy-start(s32[32]{0:T(128)} %param.17) | copy-start | bytes 388
  7.2 111.4 %all-reduce.2.cloned.1.call-start = ((), (), s32[]{:S(2)}) async-start(), calls=%async_computation.1 | async-start | bytes 8388608 | tf_op jit(solution)/shard_map/psum | solution.py:69
  11.3 281.1 %all-gather.2.cloned.1.call-start = ((), (), s32[]{:S(2)}) async-start(), calls=%async_computation.2 | async-start | bytes 9437184 | tf_op jit(solution)/shard_map/all_gather | solution.py:92
  236.4 4.5 %copy-start = (f32[1,256,1024]{2,1,0:T(8,128)S(1)}, f32[1,256,1024]{2,1,0:T(8,128)}, u32[]{:S(2)}) copy-start(f32[1,256,1024]{2,1,0:T(8,128)} %param.12) | copy-start | bytes 3145732
  236.4 4.5 %copy-start.1 = (f32[1,256,1024]{2,1,0:T(8,128)S(1)}, f32[1,256,1024]{2,1,0:T(8,128)}, u32[]{:S(2)}) copy-start(f32[1,256,1024]{2,1,0:T(8,128)} %param.11) | copy-start | bytes 3145732
Sparse Core Ops, SparseCore 0:
  12.0 106.5 all-reduce.1
  244.1 48.2 all-gather.1
where the time goes:
time: 313 us
  waiting for transfers between devices  151 us (48%)
  blocking collectives  100 us (32%)
  other arithmetic  24.4 us (8%)
  local copies, waits for them, and re-layouts  23.6 us (8%)
  between operations  14.2 us (5%)
    psum x1, waiting for transfers between devices, local(): window_sum = lax.psum(gradient.astype(jnp.float32), 'rep')  107 us
    all_to_all x1, blocking collectives, local(): lax.all_to_all(packed, 'shard', split_axis=0, concat_axis=0, tiled=True)  100 us
    all_gather x1, waiting for transfers between devices, local(): piece = lax.all_gather(updated, 'shard', axis=0, tiled=True)  44.1 us
    gather x1, local copies, waits for them, and re-layouts, packed_rows(): picked = jnp.take(gradient, window_row, axis=0)  13.9 us
    gather x1, local copies, waits for them, and re-layouts, local(): jnp.take(piece, jnp.clip(destination, 0, piece.shape[0] - 1), axis=0)  9.71 us
  transfers between devices with their start and end apart: 2, of which 2 were waited for; matrix products, arithmetic and copies ran while one was open for 2% of the time, Pallas kernels for 0%

commit v1 on v0

--- a/solution.py
+++ b/solution.py
@@ -12,6 +12,11 @@
 average_rate = 0.99
 step_count = 10.0
 reference_batch = 128.0
+
+
+def gather_and_add(value, axis):
+    pieces = lax.all_gather(value, axis)
+    return jnp.sum(pieces, axis=0)
 
 
 def optimizer_step(summed, master, moment_one, moment_two, average, decay_scale):
@@ -66,7 +71,7 @@
     slot_index = jnp.arange(owners * capacity, dtype=jnp.int32)
     dest_owner = slot_index // capacity
     dest_slot = slot_index % capacity
-    window_sum = lax.psum(gradient.astype(jnp.float32), "rep")
+    window_sum = gather_and_add(gradient.astype(jnp.float32), "rep")
     packed = packed_rows(
         window_sum,
         tensor_owner,

time: 313 us -> 601 us (1.92)
  waiting for transfers between devices: 151 us -> 416 us
  other arithmetic: 24.4 us -> 47.4 us
    all_gather x0 -> x1, waiting for transfers between devices: none -> 372 us  [gather_and_add(): pieces = lax.all_gather(value, axis)]
    psum x1 -> x0, waiting for transfers between devices: 107 us -> none  [local(): window_sum = lax.psum(gradient.astype(jnp.float32), 'rep')]
    reduce_sum x0 -> x1, other arithmetic: none -> 23 us  [gather_and_add(): return jnp.sum(pieces, axis=0)]
  transfers between devices with their start and end apart: 2 -> 2, of which waited for: 2 -> 2; matrix products, arithmetic and copies ran while one was open for 2% -> 1% of each run, Pallas kernels for 0% -> 0%
where the time goes in v1:
time: 601 us
  waiting for transfers between devices  416 us (69%)
  blocking collectives  99.7 us (17%)
  other arithmetic  47.4 us (8%)
  local copies, waits for them, and re-layouts  23.6 us (4%)
  between operations  14.2 us (2%)
    all_gather x1, waiting for transfers between devices, gather_and_add(): pieces = lax.all_gather(value, axis)  372 us
    all_to_all x1, blocking collectives, local(): lax.all_to_all(packed, 'shard', split_axis=0, concat_axis=0, tiled=True)  99.7 us
    all_gather x1, waiting for transfers between devices, local(): piece = lax.all_gather(updated, 'shard', axis=0, tiled=True)  44 us
    reduce_sum x1, other arithmetic, gather_and_add(): return jnp.sum(pieces, axis=0)  23 us
    gather x1, local copies, waits for them, and re-layouts, packed_rows(): picked = jnp.take(gradient, window_row, axis=0)  13.9 us
  transfers between devices with their start and end apart: 2, of which 2 were waited for; matrix products, arithmetic and copies ran while one was open for 1% of the time, Pallas kernels for 0%

profile of v1, /device:TPU:1, one launch (start us, length us, event | category | flops | bytes accessed | tf_op | source)
XLA Modules:
  0.0 600.7 jit_solution(15559990815617945236)
XLA Ops:
  7.2 0.0 copy-start.4
  7.2 0.0 copy-start.2
  7.2 0.0 copy-start.5
  7.2 0.0 copy-start.3
  7.2 0.0 all-gather.6.cloned.1.call-start
  7.3 4.1 convert_element_type.15
  11.3 0.0 all-gather.6.cloned.1.call-update
  11.3 0.0 all-gather.4.cloned.1.call-start
  11.4 0.0 copy-done.4
  11.4 0.0 copy-done.2
  11.4 0.0 copy-done.5
  11.4 0.0 copy-done.3
  11.5 0.2 select_reduce_fusion
  11.6 0.2 fusion.18
  11.9 371.6 %all-gather.6.cloned.1.call-done = f32[16,1,1024,1024]{3,2,1,0:T(8,128)} async-done(((f32[1,1,1024,1024]{3,2,1,0:T(8,128)}), f32[16,1,1024,1024]{3,2,1,0:T(8,128)}) %all-gather.6.cloned.1.call-update) | async-done | bytes 67108880 | tf_op jit(solution)/shard_map/all_gather | solution.py:18
  383.5 23.0 %reduce_sum.45 = f32[1024,1024]{1,0:T(8,128)} reduce(f32[16,1,1024,1024]{3,2,1,0:T(8,128)} %all-gather.6.cloned.1.call-done, f32[]{:T(128)} %constant.82.clone.1), dimensions={0,1}, to_apply=%region_3.4 | reduce | flops 15728640 | bytes 71303168 | tf_op jit(solution)/shard_map/reduce_sum | solution.py:19
  406.5 13.9 %gather_fusion = f32[2048,1024]{1,0:T(8,128)} fusion(f32[1024,1024]{1,0:T(8,128)} %reduce_sum.45, s32[2048]{0:T(1024)S(1)} %broadcast_clamp_fusion), kind=kCustom, calls=%fused_computation | custom fusion | bytes 16785408 | tf_op jit(solution)/shard_map/jit(_take)/gather | solution.py:45
  420.3 4.0 select_select_fusion
  424.3 99.7 %all_to_all.5 = f32[8,256,1024]{2,1,0:T(8,128)} all-to-all(f32[8,256,1024]{2,1,0:T(8,128)S(1)} %select_select_fusion), channel_id=1, replica_groups=mesh['rep'=16,'shard'=8] {'shard'}, dimensions={0} | all-to-all | bytes 16777216 | tf_op jit(solution)/shard_map/all_to_all | solution.py:86
  524.0 0.0 copy-start
  524.0 0.0 copy-start.1
  524.1 4.5 reduce_sum.47
  528.6 0.0 copy-done
  528.6 0.0 copy-done.1
  528.6 3.0 fusion.6
  531.6 0.0 all-gather.4.cloned.1.call-update
  531.6 0.1 select_reduce_fusion.1
  531.7 4.2 multiply_add_fusion
  536.0 44.0 %all-gather.4.cloned.1.call-done = f32[2048,1024]{1,0:T(8,128)} async-done(((f32[256,1024]{1,0:T(8,128)}), f32[2048,1024]{1,0:T(8,128)}) %all-gather.4.cloned.1.call-update) | async-done | bytes 8388624 | tf_op jit(solution)/shard_map/all_gather | solution.py:97
  580.0 9.7 %gather_fusion.1 = f32[1024,1024]{1,0:T(8,128)} fusion(f32[2048,1024]{1,0:T(8,128)} %all-gather.4.cloned.1.call-done, s32[1024]{0:T(1024)S(1)} %broadcast_clamp_fusion.1), kind=kCustom, calls=%fused_computation.1 | custom fusion | bytes 8392704 | tf_op jit(solution)/shard_map/jit(_take)/gather | solution.py:99
  589.7 4.2 select_select_fusion.1
  (11 shorter events, 0.1 us)
Async XLA Ops:
  7.2 4.2 copy-start.4
  7.2 4.2 copy-start.2
  7.2 4.2 copy-start.5
  7.2 4.2 copy-start.3
  7.2 376.3 %all-gather.6.cloned.1.call-start = ((), (), s32[]{:S(2)}) async-start(), calls=%async_computation.2 | async-start | bytes 71303168 | tf_op jit(solution)/shard_map/all_gather | solution.py:18
  11.3 568.7 %all-gather.4.cloned.1.call-start = ((), (), s32[]{:S(2)}) async-start(), calls=%async_computation.1 | async-start | bytes 9437184 | tf_op jit(solution)/shard_map/all_gather | solution.py:97
  524.0 4.5 copy-start
  524.0 4.5 copy-start.1
Sparse Core Ops, SparseCore 0:
  11.5 371.9 all-gather.5
  531.7 48.2 all-gather.3

commit v2 on v0

--- a/solution.py
+++ b/solution.py
@@ -89,7 +89,10 @@
     )
     target = tensor_owner * capacity + tensor_slot - tensor_start
     destination = jnp.sum(jnp.where(inside, target[None, :] + row_index[:, None], 0), axis=1)
-    piece = lax.all_gather(updated, "shard", axis=0, tiled=True)
+    size = lax.axis_size("shard")
+    blocks = jnp.stack([updated for _ in range(size)])
+    blocks = lax.all_to_all(blocks, "shard", split_axis=0, concat_axis=0)
+    piece = jnp.concatenate(blocks, axis=0)
     within = (destination >= 0) & (destination < piece.shape[0])
     picked = jnp.take(piece, jnp.clip(destination, 0, piece.shape[0] - 1), axis=0)
     new_params = jnp.where(within[:, None], picked, jnp.zeros((row_total, row_width), jnp.float32))

time: 313 us -> 370 us (1.18)
  waiting for transfers between devices: 151 us -> 200 us
  starting transfers between devices: 0.08 us -> 5.91 us
  local copies, waits for them, and re-layouts: 23.6 us -> 28 us
    all_to_all x0 -> x1, waiting for transfers between devices: none -> 93.7 us  [local(): blocks = lax.all_to_all(blocks, 'shard', split_axis=0, concat_axis=0)]
    all_gather x1 -> x0, waiting for transfers between devices: 44.1 us -> none  [local(): piece = lax.all_gather(updated, 'shard', axis=0, tiled=True)]
    all_to_all x0 -> x1, starting transfers between devices: none -> 5.87 us  [local(): blocks = lax.all_to_all(blocks, 'shard', split_axis=0, concat_axis=0)]
    another operation x0 -> x1, local copies, waits for them, and re-layouts: none -> 4.27 us  [local(): blocks = jnp.stack([updated for _ in range(size)])]
  transfers between devices with their start and end apart: 2 -> 2, of which waited for: 2 -> 2; matrix products, arithmetic and copies ran while one was open for 2% -> 0% of each run, Pallas kernels for 0% -> 0%
where the time goes in v2:
time: 370 us
  waiting for transfers between devices  200 us (54%)
  blocking collectives  100 us (27%)
  local copies, waits for them, and re-layouts  28 us (8%)
  other arithmetic  21.4 us (6%)
  between operations  14.2 us (4%)
  starting transfers between devices  5.91 us (2%)
    psum x1, waiting for transfers between devices, local(): window_sum = lax.psum(gradient.astype(jnp.float32), 'rep')  107 us
    all_to_all x1, blocking collectives, local(): lax.all_to_all(packed, 'shard', split_axis=0, concat_axis=0, tiled=True)  100 us
    all_to_all x1, waiting for transfers between devices, local(): blocks = lax.all_to_all(blocks, 'shard', split_axis=0, concat_axis=0)  93.7 us
    gather x1, local copies, waits for them, and re-layouts, packed_rows(): picked = jnp.take(gradient, window_row, axis=0)  13.9 us
    gather x1, local copies, waits for them, and re-layouts, local(): jnp.take(piece, jnp.clip(destination, 0, piece.shape[0] - 1), axis=0)  9.72 us
  transfers between devices with their start and end apart: 2, of which 2 were waited for; matrix products, arithmetic and copies ran while one was open for 0% of the time, Pallas kernels for 0%

profile of v2, /device:TPU:1, one launch (start us, length us, event | category | flops | bytes accessed | tf_op | source)
XLA Modules:
  0.0 369.9 jit_solution(15231252417421657724)
XLA Ops:
  7.2 0.0 copy-start.3
  7.2 0.0 copy-start.4
  7.2 0.0 copy-start.5
  7.2 0.0 copy-start.2
  7.2 0.0 all-reduce.2.cloned.1.call-start
  7.3 4.1 %bitcast_convert_fusion = f32[1024,1024]{1,0:T(8,128)} fusion(bf16[1,1,1024,1024]{3,2,1,0:T(8,128)(2,1)} %param.9), kind=kLoop, calls=%fused_computation.4 | loop fusion | flops 1048576 | bytes 6291456 | tf_op jit(solution)/shard_map/convert_element_type | solution.py:69
  11.3 0.0 all-reduce.2.cloned.1.call-update
  11.4 0.0 copy-done.3
  11.4 0.0 copy-done.4
  11.4 0.0 copy-done.5
  11.4 0.0 copy-done.2
  11.4 0.2 select_reduce_fusion
  11.6 0.2 fusion.10
  11.9 106.7 %all-reduce.2.cloned.1.call-done = f32[1024,1024]{1,0:T(8,128)} async-done(((f32[1024,1024]{1,0:T(8,128)}), f32[1024,1024]{1,0:T(8,128)}) %all-reduce.2.cloned.1.call-update) | async-done | bytes 4194320 | tf_op jit(solution)/shard_map/psum | solution.py:69
  118.6 13.9 %gather_fusion = f32[2048,1024]{1,0:T(8,128)} fusion(f32[1024,1024]{1,0:T(8,128)} %all-reduce.2.cloned.1.call-done, s32[2048]{0:T(1024)S(1)} %broadcast_clamp_fusion), kind=kCustom, calls=%fused_computation | custom fusion | bytes 16785408 | tf_op jit(solution)/shard_map/jit(_take)/gather | solution.py:40
  132.5 4.0 %select_select_fusion = f32[8,256,1024]{2,1,0:T(8,128)S(1)} fusion(f32[8,256,1024]{2,1,0:T(8,128)} %bitcast.17, pred[8,256]{1,0:T(8,128)(4,1)S(1)} %compare_and_fusion.1, pred[8,256]{1,0:T(8,128)(4,1)S(1)} %broadcast_in_dim.76), kind=kLoop, calls=%fused_computation.2 | loop fusion | flops 4194304 | bytes 16781312 | tf_op jit(solution)/shard_map/jit(_where)/select_n | solution.py:41
  136.5 100.0 %all_to_all.10 = f32[8,256,1024]{2,1,0:T(8,128)} all-to-all(f32[8,256,1024]{2,1,0:T(8,128)S(1)} %select_select_fusion), channel_id=1, replica_groups=mesh['rep'=16,'shard'=8] {'shard'}, dimensions={0} | all-to-all | bytes 16777216 | tf_op jit(solution)/shard_map/all_to_all | solution.py:81
  236.5 0.0 copy-start.1
  236.5 4.5 %reduce_sum.37 = f32[256,1024]{1,0:T(8,128)S(1)} reduce(f32[8,256,1024]{2,1,0:T(8,128)} %all_to_all.10, f32[]{:T(128)} %constant.83.clone.1), dimensions={0}, to_apply=%region_4.5 | reduce | flops 1835008 | bytes 9437188 | tf_op jit(solution)/shard_map/reduce_sum | solution.py:45
  241.0 0.0 copy-done.1
  241.0 4.2 %multiply_add_fusion = (f32[1,256,1024]{2,1,0:T(8,128)}, f32[1,256,1024]{2,1,0:T(8,128)S(1)}, f32[1,256,1024]{2,1,0:T(8,128)}, f32[1,256,1024]{2,1,0:T(8,128)}) fusion(f32[1,256,1024]{2,1,0:T(8,128)S(1)} %copy-done.1, f32[1,256,1024]{2,1,0:T(8,128)} %param.10, f32[256,1024]{1,0:T(8,128)S(1)} %reduce_sum.37, f32[1,256,1024]{2,1,0:T(8,128)} %param.11, ...), kind=kLoop, calls=%fused_computation.9 | loop fusion | flops 4456448 | bytes 9437184 | tf_op jit(solution)/shard_map/add | solution.py:24
  245.2 0.0 copy-start
  245.2 4.3 %stack.5 = f32[8,256,1024]{2,1,0:T(8,128)} broadcast(f32[256,1024]{1,0:T(8,128)S(1)} %bitcast.18), dimensions={1,2} | broadcast | bytes 9437184 | tf_op jit(solution)/shard_map/stack | solution.py:93
  249.4 0.0 copy-done
  249.4 5.9 %all-to-all-start.1 = ((f32[8,256,1024]{2,1,0:T(8,128)}), f32[8,256,1024]{2,1,0:T(8,128)}, u32[]{:S(2)}, u32[]{:S(2)}) async-start(f32[8,256,1024]{2,1,0:T(8,128)} %stack.5), calls=%async_computation.1 | async-start | bytes 16777216 | tf_op jit(solution)/shard_map/all_to_all | solution.py:94
  255.3 0.1 select_reduce_fusion.1
  255.5 93.7 %all-to-all-done.1 = f32[8,256,1024]{2,1,0:T(8,128)} async-done(((f32[8,256,1024]{2,1,0:T(8,128)}), f32[8,256,1024]{2,1,0:T(8,128)}, u32[]{:S(2)}, u32[]{:S(2)}) %all-to-all-start.1) | async-done | bytes 8388640 | tf_op jit(solution)/shard_map/all_to_all | solution.py:94
  349.2 9.7 %gather_fusion.1 = f32[1024,1024]{1,0:T(8,128)} fusion(f32[2048,1024]{1,0:T(8,128)} %bitcast.6, s32[1024]{0:T(1024)S(1)} %broadcast_clamp_fusion.1), kind=kCustom, calls=%fused_computation.1 | custom fusion | bytes 8392704 | tf_op jit(solution)/shard_map/jit(_take)/gather | solution.py:97
  358.9 4.2 %select_select_fusion.1 = f32[1024,1024]{1,0:T(8,128)} fusion(f32[1024,1024]{1,0:T(8,128)} %gather_fusion.1, pred[1024]{0:T(1024)(128)(4,1)S(1)} %get-tuple-element.10, pred[1024]{0:T(1024)(128)(4,1)S(1)} %get-tuple-element.9), kind=kLoop, calls=%fused_computation.3 | loop fusion | flops 2097152 | bytes 8390656 | tf_op jit(solution)/shard_map/jit(_where)/select_n | solution.py:98
  (11 shorter events, 0.1 us)
Async XLA Ops:
  7.2 4.2 %copy-start.3 = (s32[32]{0:T(128)S(1)}, s32[32]{0:T(128)}, u32[]{:S(2)}) copy-start(s32[32]{0:T(128)} %param.14) | copy-start | bytes 388
  7.2 4.2 %copy-start.4 = (s32[32]{0:T(128)S(1)}, s32[32]{0:T(128)}, u32[]{:S(2)}) copy-start(s32[32]{0:T(128)} %param.15) | copy-start | bytes 388
  7.2 4.2 %copy-start.5 = (s32[32]{0:T(128)S(1)}, s32[32]{0:T(128)}, u32[]{:S(2)}) copy-start(s32[32]{0:T(128)} %param.16) | copy-start | bytes 388
  7.2 4.2 %copy-start.2 = (s32[32]{0:T(128)S(1)}, s32[32]{0:T(128)}, u32[]{:S(2)}) copy-start(s32[32]{0:T(128)} %param.17) | copy-start | bytes 388
  7.2 111.4 %all-reduce.2.cloned.1.call-start = ((), (), s32[]{:S(2)}) async-start(), calls=%async_computation.2 | async-start | bytes 8388608 | tf_op jit(solution)/shard_map/psum | solution.py:69
  236.5 4.5 %copy-start.1 = (f32[1,256,1024]{2,1,0:T(8,128)S(1)}, f32[1,256,1024]{2,1,0:T(8,128)}, u32[]{:S(2)}) copy-start(f32[1,256,1024]{2,1,0:T(8,128)} %param.13) | copy-start | bytes 3145732
  245.2 4.3 %copy-start = (f32[1,256,1024]{2,1,0:T(8,128)}, f32[1,256,1024]{2,1,0:T(8,128)S(1)}, u32[]{:S(2)}) copy-start(f32[1,256,1024]{2,1,0:T(8,128)S(1)} %get-tuple-element.6) | copy-start | bytes 3145732
  249.4 99.7 %all-to-all-start.1 = ((f32[8,256,1024]{2,1,0:T(8,128)}), f32[8,256,1024]{2,1,0:T(8,128)}, u32[]{:S(2)}, u32[]{:S(2)}) async-start(f32[8,256,1024]{2,1,0:T(8,128)} %stack.5), calls=%async_computation.1 | async-start | bytes 16777216 | tf_op jit(solution)/shard_map/all_to_all | solution.py:94
Sparse Core Ops, SparseCore 0:
  12.0 106.5 all-reduce.1
